TPU v7x, 32 devices: a whole 2x2x4 slice. The times are simulated.
32 devices in a mesh: grp: 1, dev: 32 (over z, y, x, core).
Axes of the slice: x: 2, y: 2, z: 4, core: 2. Of those that a mesh axis runs over, the one named last changes fastest.
Arguments:
- hidden_in: bfloat16 [640, 32, 768], P(('grp', 'dev')), may hold values from -6 to 6
- grad_out: bfloat16 [640, 32, 768], P(('grp', 'dev')), may hold values from -6 to 6
- norm_gain: float32 [768], replicated, may hold values from 0.25 to 1.75
- w_qkv: bfloat16 [768, 2304], replicated, may hold values from -0.21875 to 0.21875
- w_out: bfloat16 [768, 768], replicated, may hold values from -0.21875 to 0.21875
- sharpness: float32 [12], replicated, may hold values from 4 to 20
- cohort_ids: int32 [640], P('grp'), may hold values from 0 to 3
- observed: int32 [640, 32], P('grp', 'dev'), may hold values 0 or 1
Outputs:
- grad_in: bfloat16 [640, 32, 768], P(('grp', 'dev'))
- grad_qkv: float32 [768, 2304], P(('grp', 'dev'))
- grad_wout: float32 [768, 768], P(('grp', 'dev'))
All inputs are finite; a program needn't handle non-finite values. No bound on the sum of `observed` on one device may be relied on, other than what follows from the above.
Results may differ from a plain program's by a relative error of at most 0.015.
Values may be sent and summed in bfloat16 or wider, within the bound.
A program may use at most 128 MiB of HBM per device.

v0:
```python
import jax
import jax.numpy as jnp
from jax import lax
from jax.sharding import PartitionSpec as P

epsilon = 1e-06


def row_sum(left, right):
    return lax.dot_general(
        left, right, (((0,), (0,)), ((), ())), preferred_element_type=jnp.float32
    )


def forward_part(rows_in, norm_gain, w_qkv, heads):
    campaigns, patches, width = rows_in.shape
    head_size = width // heads
    values = rows_in.astype(jnp.float32)
    inv_rms = lax.rsqrt(jnp.mean(values * values, axis=-1, keepdims=True) + epsilon)
    unit_rows = values * inv_rms
    normed = (unit_rows * norm_gain).astype(jnp.bfloat16).reshape(-1, width)
    projected = jnp.dot(normed, w_qkv, preferred_element_type=jnp.float32)
    shape4 = (campaigns, patches, heads, head_size)
    query_raw = projected[:, :width].reshape(shape4)
    key_raw = projected[:, width : 2 * width].reshape(shape4)
    value_half = projected[:, 2 * width :].reshape(shape4).astype(jnp.bfloat16)
    query_inv = lax.rsqrt(jnp.mean(query_raw * query_raw, axis=-1, keepdims=True) + epsilon)
    key_inv = lax.rsqrt(jnp.mean(key_raw * key_raw, axis=-1, keepdims=True) + epsilon)
    query_unit = query_raw * query_inv
    key_unit = key_raw * key_inv
    return (
        inv_rms,
        unit_rows,
        normed,
        query_unit,
        query_inv,
        key_unit,
        key_inv,
        query_unit.astype(jnp.bfloat16),
        key_unit.astype(jnp.bfloat16),
        value_half,
    )


def body(hidden_in, grad_out, norm_gain, w_qkv, w_out, sharpness, cohort_ids, observed):
    heads = sharpness.shape[0]
    rows_in, grad_rows = (
        lax.all_to_all(hidden_in, "dev", split_axis=1, concat_axis=0, tiled=True),
        lax.all_to_all(grad_out, "dev", split_axis=1, concat_axis=0, tiled=True),
    )
    forward = forward_part(rows_in, norm_gain, w_qkv, heads)
    (
        inv_rms,
        unit_rows,
        normed,
        query_unit,
        query_inv,
        key_unit,
        key_inv,
        query_half,
        key_half,
        value_half,
    ) = forward
    campaigns, patches, width = rows_in.shape
    head_size = width // heads
    shape4 = (campaigns, patches, heads, head_size)
    dy_rows = grad_rows.reshape(-1, width)
    grad_attn = lax.dot_general(
        dy_rows, w_out, (((1,), (1,)), ((), ())), preferred_element_type=jnp.float32
    )
    grad_attn = grad_attn.astype(jnp.bfloat16).reshape(shape4)
    same = cohort_ids[:, None] == cohort_ids[None, :]
    diagonal = jnp.eye(campaigns, dtype=bool)
    keys_seen = (observed.T == 1)[:, None, :]
    allowed = jnp.where(same[None] & (keys_seen | diagonal[None]), 1.0, 0.0).astype(jnp.float32)

    def head_step(index, carry):
        attended, grad_qunit, grad_kunit, grad_value = carry
        query_head = lax.dynamic_index_in_dim(query_half, index, 2, keepdims=False)
        key_head = lax.dynamic_index_in_dim(key_half, index, 2, keepdims=False)
        value_head = lax.dynamic_index_in_dim(value_half, index, 2, keepdims=False)
        grad_head = lax.dynamic_index_in_dim(grad_attn, index, 2, keepdims=False)
        scale = lax.dynamic_index_in_dim(sharpness, index, 0, keepdims=False) / head_size
        scores = (
            jnp.einsum("ipe,jpe->pij", query_head, key_head, preferred_element_type=jnp.float32)
            * scale
        )
        raw_weights = jnp.exp(scores) * allowed
        probs = raw_weights / jnp.sum(raw_weights, axis=-1, keepdims=True)
        probs_half = probs.astype(jnp.bfloat16)
        out_head = jnp.einsum(
            "pij,jpe->ipe", probs_half, value_head, preferred_element_type=jnp.float32
        )
        grad_probs = jnp.einsum(
            "ipe,jpe->pij", grad_head, value_head, preferred_element_type=jnp.float32
        )
        value_grad = jnp.einsum(
            "pij,ipe->jpe", probs_half, grad_head, preferred_element_type=jnp.float32
        )
        row_dot = jnp.sum(grad_probs * probs, axis=-1, keepdims=True)
        grad_scores = (probs * (grad_probs - row_dot) * scale).astype(jnp.bfloat16)
        qunit_head = jnp.einsum(
            "pij,jpe->ipe", grad_scores, key_head, preferred_element_type=jnp.float32
        )
        kunit_head = jnp.einsum(
            "pij,ipe->jpe", grad_scores, query_head, preferred_element_type=jnp.float32
        )
        return (
            lax.dynamic_update_index_in_dim(attended, out_head, index, 2),
            lax.dynamic_update_index_in_dim(grad_qunit, qunit_head, index, 2),
            lax.dynamic_update_index_in_dim(grad_kunit, kunit_head, index, 2),
            lax.dynamic_update_index_in_dim(grad_value, value_grad, index, 2),
        )

    empty = jnp.zeros(shape4, jnp.float32)
    attended, grad_qunit, grad_kunit, grad_value = lax.fori_loop(
        0, heads, head_step, (empty, empty, empty, empty)
    )
    grad_query = query_inv * (
        grad_qunit - query_unit * jnp.mean(grad_qunit * query_unit, axis=-1, keepdims=True)
    )
    grad_key = key_inv * (
        grad_kunit - key_unit * jnp.mean(grad_kunit * key_unit, axis=-1, keepdims=True)
    )
    grad_proj = jnp.concatenate(
        [grad_query.reshape(-1, width), grad_key.reshape(-1, width), grad_value.reshape(-1, width)],
        axis=1,
    ).astype(jnp.bfloat16)
    attended_half = attended.astype(jnp.bfloat16).reshape(-1, width)
    out_term = row_sum(attended_half, dy_rows)
    grad_wout = lax.psum_scatter(
        out_term.astype(jnp.bfloat16), "dev", scatter_dimension=0, tiled=True
    ).astype(jnp.float32)
    grad_normed = lax.dot_general(
        grad_proj, w_qkv, (((1,), (1,)), ((), ())), preferred_element_type=jnp.float32
    )
    shaped = grad_normed.reshape(campaigns, patches, width) * norm_gain
    result = grad_rows.astype(jnp.float32) + inv_rms * (
        shaped - unit_rows * jnp.mean(shaped * unit_rows, axis=-1, keepdims=True)
    )
    grad_in = lax.all_to_all(
        result.astype(jnp.bfloat16), "dev", split_axis=0, concat_axis=1, tiled=True
    )
    grad_qkv = lax.psum_scatter(
        row_sum(normed, grad_proj).astype(jnp.bfloat16), "dev", scatter_dimension=0, tiled=True
    ).astype(jnp.float32)
    return (grad_in, grad_qkv, grad_wout)


def solution(mesh):
    in_specs = (
        P(("grp", "dev"), None, None),
        P(("grp", "dev"), None, None),
        P(),
        P(),
        P(),
        P(),
        P("grp"),
        P("grp", "dev"),
    )
    out_specs = (P(("grp", "dev"), None, None), P(("grp", "dev"), None), P(("grp", "dev"), None))
    return jax.shard_map(body, mesh=mesh, in_specs=in_specs, out_specs=out_specs, check_vma=False)
```

profile of v0, /device:TPU:0, one launch (start us, length us, event | category | flops | bytes accessed | tf_op | source)
XLA Modules:
  0.0 459.8 jit_solution(5012240428037647978)
XLA Ops:
  7.2 2.9 copy.28
  10.1 7.4 %all-to-all-start.1 = ((bf16[20,32,768]{2,0,1:T(8,128)(2,1)}), bf16[20,32,768]{2,0,1:T(8,128)(2,1)}, u32[]{:S(2)}, u32[]{:S(2)}) async-start(bf16[20,32,768]{2,0,1:T(8,128)(2,1)} %copy.28), calls=%async_computation.1 | async-start | bytes 2359296 | tf_op jit(solution)/shard_map/all_to_all | solution.py:48
  17.6 2.8 copy.27
  21.0 25.6 %all-to-all-done.1 = bf16[20,32,768]{2,0,1:T(8,128)(2,1)} async-done(((bf16[20,32,768]{2,0,1:T(8,128)(2,1)}), bf16[20,32,768]{2,0,1:T(8,128)(2,1)}, u32[]{:S(2)}, u32[]{:S(2)}) %all-to-all-start.1) | async-done | bytes 983072 | tf_op jit(solution)/shard_map/all_to_all | solution.py:48
  46.5 3.7 all-to-all-start
  52.6 2.9 convert_bitcast_fusion
  56.1 2.7 reshape.437
  60.3 4.1 fusion.38
  65.4 2.3 fusion.40
  67.7 2.9 copy.33
  70.5 2.9 copy.31
  73.4 2.2 copy.32
  75.6 1.9 multiply_reduce_fusion.4
  79.3 2.1 all_to_all.36
  81.4 3.5 convolution_convert_fusion.2
  85.0 2.2 copy.34
  87.2 3.9 multiply_convert_fusion.4
  91.1 145.6 %while.20 = (s32[]{:T(128)}, bf16[640,1,12,64]{0,3,2,1:T(8,128)(2,1)}, f32[640,1,12,64]{0,3,2,1:T(8,128)}, f32[640,1,12,64]{0,3,2,1:T(8,128)}, bf16[640,1,12,64]...) while((s32[]{:T(128)}, ...), condition=%wide.region_6.7_spmd.clone, body=%wide.region_3.6_spmd.clone.sunk | while | flops 322763520 | bytes 15271073 | solution.py:116
  95.8 1.9 fusion.73
  97.8 1.8 fusion.72
  99.6 1.9 fusion.74
  108.0 1.9 fusion.73
  111.7 1.9 fusion.74
  120.1 1.9 fusion.73
  122.0 1.8 fusion.72
  123.9 1.9 fusion.74
  132.2 1.9 fusion.73
  134.2 1.8 fusion.72
  136.0 1.9 fusion.74
  144.3 1.9 fusion.73
  148.1 1.9 fusion.74
  156.5 1.9 fusion.73
  158.4 1.8 fusion.72
  160.2 1.9 fusion.74
  168.6 1.9 fusion.73
  172.4 1.9 fusion.74
  180.7 2.0 fusion.73
  182.7 1.8 fusion.72
  184.5 1.9 fusion.74
  192.9 1.9 fusion.73
  194.8 1.8 fusion.72
  196.6 1.9 fusion.74
  205.0 1.9 fusion.73
  208.8 1.9 fusion.74
  217.1 1.9 fusion.73
  219.1 1.8 fusion.72
  220.9 1.9 fusion.74
  229.3 1.9 fusion.73
  231.2 1.8 fusion.72
  233.0 1.9 fusion.74
  236.8 3.2 multiply_reduce_fusion.3
  241.3 3.3 convolution_convert_fusion.1
  246.4 2.7 multiply_convert_fusion.2
  252.0 6.2 %convolution_convert_fusion = bf16[768,2304]{1,0:T(8,128)(2,1)} fusion(bf16[640,768]{0,1:T(8,128)(2,1)} %bitcast.11, bf16[640,768]{0,1:T(8,128)(2,1)S(1)} %bitcast.138, bf16[640,768]{0,1:T(8,128)(2,1)S(1)} %bitcast.136, f32[640,768]{1,0:T(8,128)S(1)} %copy-done.4, f32[768]{0:T(1024)S(1)} %copy-done.16, f32[640]{0:T(1024)S(1)} %copy-done.15), kind=kOutput, calls=%fused_computation.41 | convolution fusion | flops 2277015552 | bytes 8459776 | tf_op jit(solution)/shard_map/dot_general | solution.py:10
  258.3 5.5 %multiply_reduce_fusion.1 = (f32[640]{0:T(1024)S(1)}, f32[640,768]{1,0:T(8,128)S(1)}) fusion(f32[640,768]{1,0:T(8,128)} %reshape.437, f32[768]{0:T(1024)S(1)} %copy-done.16, f32[640]{0:T(1024)S(1)} %copy-done.15, bf16[768,2304]{1,0:T(8,128)(2,1)S(1)} %copy-done, bf16[640,768]{0,1:T(8,128)(2,1)} %bitcast.11, bf16[640,768]{0,1:T(8,128)(2,1)} %bitcast.139, ...), kind=kOutput, calls=%fused_computation.48 | convolution fusion | flops 2275737088 | bytes 10428416 | tf_op jit(solution)/shard_map/dot_general | solution.py:134
  265.8 3.3 reduce.21
  269.0 3.3 reshape.446
  272.3 6.0 %all-to-all-start.2 = ((bf16[32,2,7680]{2,1,0:T(2,128)(2,1)}), bf16[32,2,7680]{2,1,0:T(2,128)(2,1)}, u32[]{:S(2)}, u32[]{:S(2)}) async-start(bf16[32,2,7680]{2,1,0:T(2,128)(2,1)} %reshape.446), calls=%async_computation.2 | async-start | bytes 1966080 | tf_op jit(solution)/shard_map/all_to_all | solution.py:141
  278.3 65.1 %reduce-scatter.5.cloned.1.call-done = bf16[24,768]{1,0:T(8,128)(2,1)} async-done(((bf16[768,768]{1,0:T(8,128)(2,1)}), bf16[24,768]{1,0:T(8,128)(2,1)}) %reduce-scatter.5.cloned.1.call-update) | async-done | bytes 36880 | tf_op jit(solution)/shard_map/reduce_scatter | solution.py:131
  344.8 5.6 %reshape.447 = bf16[640,1,768]{2,1,0:T(2,128)(2,1)} reshape(bf16[32,2,7680]{2,1,0:T(2,128)(2,1)} %all-to-all-done.2) | data formatting | bytes 1966080
  350.5 7.9 %reduce.19 = bf16[640,768]{1,0:T(8,128)(2,1)} reduce(bf16[640,1,768]{2,1,0:T(2,128)(2,1)} %reshape.447, bf16[]{:T(256)} %constant.84), dimensions={1}, to_apply=%all_to_all.38.reduce_sub_computation | reduce | bytes 1966082 | tf_op jit(solution)/shard_map/all_to_all | solution.py:141
  358.4 2.2 all_to_all.39
  360.6 2.4 copy.36
  363.0 88.4 %reduce-scatter.3.cloned.1.call-done = bf16[24,2304]{1,0:T(8,128)(2,1)} async-done(((bf16[768,2304]{1,0:T(8,128)(2,1)}), bf16[24,2304]{1,0:T(8,128)(2,1)}) %reduce-scatter.3.cloned.1.call-update) | async-done | bytes 110608 | tf_op jit(solution)/shard_map/reduce_scatter | solution.py:144
  (135 shorter events, 95.8 us)
Async XLA Ops:
  7.2 53.1 %copy-start = (bf16[768,2304]{1,0:T(8,128)(2,1)S(1)}, bf16[768,2304]{1,0:T(8,128)(2,1)}, u32[]{:S(2)}) copy-start(bf16[768,2304]{1,0:T(8,128)(2,1)} %param.13) | copy-start | bytes 10616836
  10.1 10.3 %copy-start.17 = (s32[640,1]{0,1:T(1,128)S(1)}, s32[640,1]{0,1:T(1,128)}, u32[]{:S(2)}) copy-start(s32[640,1]{0,1:T(1,128)} %param.17) | copy-start | bytes 7684
  10.1 36.5 %all-to-all-start.1 = ((bf16[20,32,768]{2,0,1:T(8,128)(2,1)}), bf16[20,32,768]{2,0,1:T(8,128)(2,1)}, u32[]{:S(2)}, u32[]{:S(2)}) async-start(bf16[20,32,768]{2,0,1:T(8,128)(2,1)} %copy.28), calls=%async_computation.1 | async-start | bytes 2359296 | tf_op jit(solution)/shard_map/all_to_all | solution.py:48
  46.5 32.7 %all-to-all-start = ((bf16[20,32,768]{2,0,1:T(8,128)(2,1)}), bf16[20,32,768]{2,0,1:T(8,128)(2,1)}, u32[]{:S(2)}, u32[]{:S(2)}) async-start(bf16[20,32,768]{2,0,1:T(8,128)(2,1)} %copy.27), calls=%async_computation | async-start | bytes 2359296 | tf_op jit(solution)/shard_map/all_to_all | solution.py:49
  50.3 293.1 %reduce-scatter.5.cloned.1.call-start = ((), (), s32[]{:S(2)}) async-start(), calls=%async_computation.6 | async-start | bytes 1216512 | tf_op jit(solution)/shard_map/reduce_scatter | solution.py:131
  52.6 2.9 copy-start.14
  75.6 2.1 copy-start.3
  87.2 3.9 copy-start.18
  87.2 3.9 copy-start.19
  87.2 3.9 copy-start.20
  236.7 3.2 copy-start.1
  236.8 3.3 copy-start.6
  236.8 3.3 copy-start.12
  240.1 1.2 copy-start.8
  244.6 206.7 %reduce-scatter.3.cloned.1.call-start = ((), (), s32[]{:S(2)}) async-start(), calls=%async_computation.5 | async-start | bytes 3649536 | tf_op jit(solution)/shard_map/reduce_scatter | solution.py:144
  246.4 2.7 copy-start.2
  246.4 3.3 copy-start.7
  246.4 3.3 copy-start.13
  249.8 1.0 copy-start.10
  249.8 2.3 copy-start.4
  249.8 2.3 copy-start.15
  249.8 2.3 copy-start.16
  250.2 0.9 copy-start.11
  258.2 5.5 %copy-start.5 = (f32[640,768]{1,0:T(8,128)S(1)}, f32[640,768]{1,0:T(8,128)}, u32[]{:S(2)}) copy-start(f32[640,768]{1,0:T(8,128)} %reshape.437) | copy-start | bytes 5898244
  258.2 5.5 %copy-start.9 = (bf16[640,768]{1,0:T(8,128)(2,1)S(1)}, bf16[640,768]{1,0:T(8,128)(2,1)}, u32[]{:S(2)}) copy-start(bf16[640,768]{1,0:T(8,128)(2,1)} %all_to_all.36) | copy-start | bytes 2949124
  272.3 72.6 %all-to-all-start.2 = ((bf16[32,2,7680]{2,1,0:T(2,128)(2,1)}), bf16[32,2,7680]{2,1,0:T(2,128)(2,1)}, u32[]{:S(2)}, u32[]{:S(2)}) async-start(bf16[32,2,7680]{2,1,0:T(2,128)(2,1)} %reshape.446), calls=%async_computation.2 | async-start | bytes 1966080 | tf_op jit(solution)/shard_map/all_to_all | solution.py:141
Sparse Core Ops, SparseCore 0:
  244.8 98.6 reduce-scatter.4
  348.8 102.4 reduce-scatter.2
where the time goes:
time: 464 us; the launch traced here: 460 us
  waiting for transfers between devices  179 us (39%)
  matrix products  149 us (32%)
  local copies, waits for them, and re-layouts  50.9 us (11%)
  other arithmetic  41.2 us (9%)
  starting transfers between devices  17.5 us (4%)
  between operations  14.2 us (3%)
  loops' own time  7.86 us (2%)
    reduce_scatter x1, waiting for transfers between devices, body(): lax.psum_scatter(row_sum(normed, grad_proj).astype(jnp.bfloat16), 'dev',...  88.4 us
    reduce_scatter x1, waiting for transfers between devices, body(): lax.psum_scatter(out_term.astype(jnp.bfloat16), 'dev', scatter_dimension=...  65.1 us
    all_to_all x1, waiting for transfers between devices, body(): lax.all_to_all(hidden_in, 'dev', split_axis=1, concat_axis=0, tiled=True)  25.6 us
    dot_general x12, matrix products, head_step(): jnp.einsum('pij,ipe->jpe', grad_scores, query_head, preferred_element_typ...  23.3 us
    dot_general x12, matrix products, head_step(): jnp.einsum('pij,ipe->jpe', probs_half, grad_head, preferred_element_type=...  22.9 us
    dot_general x12, matrix products, head_step(): jnp.einsum('pij,jpe->ipe', grad_scores, key_head, preferred_element_type=...  21.9 us
    dot_general x12, matrix products, head_step(): jnp.einsum('pij,jpe->ipe', probs_half, value_head, preferred_element_type...  21.6 us
    unnamed x48, local copies, waits for them, and re-layouts  20.8 us
  transfers between devices with their start and end apart: 5, of which 4 were waited for; matrix products, arithmetic and copies ran while one was open for 16% of the time, Pallas kernels for 0%

commit v1 on v0

--- a/solution.py
+++ b/solution.py
@@ -4,6 +4,12 @@
 from jax.sharding import PartitionSpec as P
 
 epsilon = 1e-06
+
+
+def exchange_blocks(x, axis, split, join):
+    pieces = jnp.split(x, lax.axis_size(axis), axis=split)
+    arrived = lax.all_to_all(jnp.stack(pieces), axis, 0, 0)
+    return jnp.concatenate(arrived, axis=join)
 
 
 def row_sum(left, right):
@@ -45,7 +51,7 @@
 def body(hidden_in, grad_out, norm_gain, w_qkv, w_out, sharpness, cohort_ids, observed):
     heads = sharpness.shape[0]
     rows_in, grad_rows = (
-        lax.all_to_all(hidden_in, "dev", split_axis=1, concat_axis=0, tiled=True),
+        exchange_blocks(hidden_in, "dev", 1, 0),
         lax.all_to_all(grad_out, "dev", split_axis=1, concat_axis=0, tiled=True),
     )
     forward = forward_part(rows_in, norm_gain, w_qkv, heads)

time: 464 us -> 491 us (1.058)
  local copies, waits for them, and re-layouts: 50.9 us -> 78.6 us
  waiting for transfers between devices: 179 us -> 184 us
    unnamed x48 -> x75, local copies, waits for them, and re-layouts: 20.8 us -> 36.5 us
    dynamic_slice x12, local copies, waits for them, and re-layouts: 7.6 us -> 15.4 us  [head_step(): lax.dynamic_index_in_dim(sharpness, index, 0, keepdims=False) / head_size]
    all_to_all x1, waiting for transfers between devices: 0.09 us -> 5.06 us  [body(): lax.all_to_all(grad_out, 'dev', split_axis=1, concat_axis=0, tiled=True)]
  transfers between devices with their start and end apart: 5 -> 5, of which waited for: 4 -> 4; matrix products, arithmetic and copies ran while one was open for 16% -> 14% of each run, Pallas kernels for 0% -> 0%
where the time goes in v1:
time: 491 us; the launch traced here: 487 us
  waiting for transfers between devices  184 us (37%)
  matrix products  149 us (30%)
  local copies, waits for them, and re-layouts  78.6 us (16%)
  other arithmetic  37.7 us (8%)
  starting transfers between devices  15.6 us (3%)
  between operations  14.3 us (3%)
  loops' own time  7.84 us (2%)
    reduce_scatter x1, waiting for transfers between devices, body(): lax.psum_scatter(row_sum(normed, grad_proj).astype(jnp.bfloat16), 'dev',...  88.4 us
    reduce_scatter x1, waiting for transfers between devices, body(): lax.psum_scatter(out_term.astype(jnp.bfloat16), 'dev', scatter_dimension=...  65.1 us
    unnamed x75, local copies, waits for them, and re-layouts  36.5 us
    all_to_all x1, waiting for transfers between devices, exchange_blocks(): arrived = lax.all_to_all(jnp.stack(pieces), axis, 0, 0)  25.6 us
    dot_general x12, matrix products, head_step(): jnp.einsum('pij,ipe->jpe', grad_scores, query_head, preferred_element_typ...  23.3 us
    dot_general x12, matrix products, head_step(): jnp.einsum('pij,ipe->jpe', probs_half, grad_head, preferred_element_type=...  22.9 us
    dot_general x12, matrix products, head_step(): jnp.einsum('pij,jpe->ipe', grad_scores, key_head, preferred_element_type=...  21.8 us
    dot_general x12, matrix products, head_step(): jnp.einsum('pij,jpe->ipe', probs_half, value_head, preferred_element_type...  21.6 us
  transfers between devices with their start and end apart: 5, of which 4 were waited for; matrix products, arithmetic and copies ran while one was open for 14% of the time, Pallas kernels for 0%

profile of v1, /device:TPU:0, one launch (start us, length us, event | category | flops | bytes accessed | tf_op | source)
XLA Modules:
  0.0 487.0 jit_solution(8816637736598797060)
XLA Ops:
  7.2 3.6 fusion.41
  31.6 7.4 %all-to-all-start.1 = ((bf16[32,20,1,768]{3,1,2,0:T(8,128)(2,1)}), bf16[32,20,1,768]{3,1,2,0:T(8,128)(2,1)}, u32[]{:S(2)}, u32[]{:S(2)}) async-start(bf16[32,20,1,768]{3,1,2,0:T(8,128)(2,1)} %constant_dynamic-update-slice_fusion), calls=%async_computation.1 | async-start | bytes 2359296 | tf_op jit(solution)/shard_map/all_to_all | solution.py:11
  39.1 2.8 copy.88
  42.4 25.6 %all-to-all-done.1 = bf16[32,20,1,768]{3,1,2,0:T(8,128)(2,1)} async-done(((bf16[32,20,1,768]{3,1,2,0:T(8,128)(2,1)}), bf16[32,20,1,768]{3,1,2,0:T(8,128)(2,1)}, u32[]{:S(2)}, u32[]{:S(2)}) %all-to-all-start.1) | async-done | bytes 983072 | tf_op jit(solution)/shard_map/all_to_all | solution.py:11
  68.0 3.7 all-to-all-start
  74.3 2.5 reshape.434
  76.8 4.1 fusion.37
  81.9 2.3 fusion.39
  84.2 2.9 copy.123
  87.0 2.9 copy.121
  89.9 2.2 copy.122
  92.1 1.9 multiply_reduce_fusion.5
  95.7 5.1 %all-to-all-done = bf16[20,32,768]{2,0,1:T(8,128)(2,1)} async-done(((bf16[20,32,768]{2,0,1:T(8,128)(2,1)}), bf16[20,32,768]{2,0,1:T(8,128)(2,1)}, u32[]{:S(2)}, u32[]{:S(2)}) %all-to-all-start) | async-done | bytes 983072 | tf_op jit(solution)/shard_map/all_to_all | solution.py:55
  100.8 2.1 all_to_all.32
  102.9 3.5 convolution_convert_fusion.2
  106.4 2.2 copy.124
  108.7 3.9 multiply_convert_fusion.4
  112.6 153.4 %while.20 = (s32[]{:T(128)}, bf16[640,1,12,64]{0,3,2,1:T(8,128)(2,1)}, f32[640,1,12,64]{0,3,2,1:T(8,128)}, f32[640,1,12,64]{0,3,2,1:T(8,128)}, bf16[640,1,12,64]...) while((s32[]{:T(128)}, ...), condition=%wide.region_6.7_spmd.clone, body=%wide.region_3.6_spmd.clone.sunk | while | flops 322763520 | bytes 15271073 | solution.py:122
  117.9 1.9 fusion.74
  121.7 1.9 fusion.75
  130.7 1.9 fusion.74
  134.4 1.9 fusion.75
  143.5 1.9 fusion.74
  147.2 1.9 fusion.75
  156.2 1.9 fusion.74
  158.2 1.8 fusion.73
  160.0 1.9 fusion.75
  169.0 1.9 fusion.74
  170.9 1.8 fusion.73
  172.8 1.9 fusion.75
  181.8 2.0 fusion.74
  183.7 1.9 fusion.73
  185.6 1.9 fusion.75
  194.6 1.9 fusion.74
  198.3 1.9 fusion.75
  207.4 1.9 fusion.74
  209.3 1.8 fusion.73
  211.1 1.9 fusion.75
  220.2 1.9 fusion.74
  222.1 1.8 fusion.73
  223.9 1.9 fusion.75
  232.9 1.9 fusion.74
  234.9 1.8 fusion.73
  236.7 1.9 fusion.75
  245.7 1.9 fusion.74
  247.6 1.8 fusion.73
  249.5 1.9 fusion.75
  258.5 1.9 fusion.74
  260.4 1.8 fusion.73
  262.3 1.9 fusion.75
  266.0 3.2 multiply_reduce_fusion.4
  270.5 3.3 convolution_convert_fusion.1
  275.7 2.7 multiply_convert_fusion.2
  281.3 6.2 %convolution_convert_fusion = bf16[768,2304]{1,0:T(8,128)(2,1)} fusion(bf16[640,768]{0,1:T(8,128)(2,1)} %bitcast.40, bf16[640,768]{0,1:T(8,128)(2,1)S(1)} %bitcast.260, bf16[640,768]{0,1:T(8,128)(2,1)S(1)} %bitcast.258, f32[640,768]{1,0:T(8,128)S(1)} %copy-done.4, f32[768]{0:T(1024)S(1)} %copy-done.16, f32[640]{0:T(1024)S(1)} %copy-done.15), kind=kOutput, calls=%fused_computation.41 | convolution fusion | flops 2277015552 | bytes 8459776 | tf_op jit(solution)/shard_map/dot_general | solution.py:16
  287.5 5.5 %multiply_reduce_fusion.2 = (f32[640]{0:T(1024)S(1)}, f32[640,768]{1,0:T(8,128)S(1)}) fusion(f32[640,768]{1,0:T(8,128)} %reshape.434, f32[768]{0:T(1024)S(1)} %copy-done.16, f32[640]{0:T(1024)S(1)} %copy-done.15, bf16[768,2304]{1,0:T(8,128)(2,1)S(1)} %copy-done, bf16[640,768]{0,1:T(8,128)(2,1)} %bitcast.40, bf16[640,768]{0,1:T(8,128)(2,1)} %bitcast.261, ...), kind=kOutput, calls=%fused_computation.46 | convolution fusion | flops 2275737088 | bytes 10428416 | tf_op jit(solution)/shard_map/dot_general | solution.py:140
  295.0 3.2 reduce.19
  298.3 3.3 reshape.442
  301.6 4.0 all-to-all-start.2
  305.5 65.1 %reduce-scatter.5.cloned.1.call-done = bf16[24,768]{1,0:T(8,128)(2,1)} async-done(((bf16[768,768]{1,0:T(8,128)(2,1)}), bf16[24,768]{1,0:T(8,128)(2,1)}) %reduce-scatter.5.cloned.1.call-update) | async-done | bytes 36880 | tf_op jit(solution)/shard_map/reduce_scatter | solution.py:137
  372.0 5.6 %reshape.443 = bf16[640,1,768]{2,1,0:T(2,128)(2,1)} reshape(bf16[32,2,7680]{2,1,0:T(2,128)(2,1)} %all-to-all-done.2) | data formatting | bytes 1966080
  377.7 7.9 %reduce.17 = bf16[640,768]{1,0:T(8,128)(2,1)} reduce(bf16[640,1,768]{2,1,0:T(2,128)(2,1)} %reshape.443, bf16[]{:T(256)} %constant.84), dimensions={1}, to_apply=%all_to_all.34.reduce_sub_computation | reduce | bytes 1966082 | tf_op jit(solution)/shard_map/all_to_all | solution.py:147
  385.6 2.2 all_to_all.35
  387.7 2.4 copy.126
  390.2 88.4 %reduce-scatter.3.cloned.1.call-done = bf16[24,2304]{1,0:T(8,128)(2,1)} async-done(((bf16[768,2304]{1,0:T(8,128)(2,1)}), bf16[24,2304]{1,0:T(8,128)(2,1)}) %reduce-scatter.3.cloned.1.call-update) | async-done | bytes 110608 | tf_op jit(solution)/shard_map/reduce_scatter | solution.py:150
  (163 shorter events, 122.5 us)
Async XLA Ops:
  7.2 69.6 %copy-start = (bf16[768,2304]{1,0:T(8,128)(2,1)S(1)}, bf16[768,2304]{1,0:T(8,128)(2,1)}, u32[]{:S(2)}) copy-start(bf16[768,2304]{1,0:T(8,128)(2,1)} %param.13) | copy-start | bytes 10616836
  7.2 3.6 copy-start.10
  31.6 36.5 %all-to-all-start.1 = ((bf16[32,20,1,768]{3,1,2,0:T(8,128)(2,1)}), bf16[32,20,1,768]{3,1,2,0:T(8,128)(2,1)}, u32[]{:S(2)}, u32[]{:S(2)}) async-start(bf16[32,20,1,768]{3,1,2,0:T(8,128)(2,1)} %constant_dynamic-update-slice_fusion), calls=%async_computation.1 | async-start | bytes 2359296 | tf_op jit(solution)/shard_map/all_to_all | solution.py:11
  39.0 2.8 copy-start.17
  68.0 32.7 %all-to-all-start = ((bf16[20,32,768]{2,0,1:T(8,128)(2,1)}), bf16[20,32,768]{2,0,1:T(8,128)(2,1)}, u32[]{:S(2)}, u32[]{:S(2)}) async-start(bf16[20,32,768]{2,0,1:T(8,128)(2,1)} %copy.88), calls=%async_computation | async-start | bytes 2359296 | tf_op jit(solution)/shard_map/all_to_all | solution.py:55
  71.8 298.8 %reduce-scatter.5.cloned.1.call-start = ((), (), s32[]{:S(2)}) async-start(), calls=%async_computation.6 | async-start | bytes 1216512 | tf_op jit(solution)/shard_map/reduce_scatter | solution.py:137
  74.3 2.5 copy-start.15
  74.3 2.5 copy-start.16
  92.1 2.1 copy-start.3
  108.7 3.9 copy-start.18
  108.7 3.9 copy-start.19
  266.0 3.2 copy-start.1
  266.0 3.3 copy-start.6
  266.0 3.3 copy-start.13
  269.3 1.2 copy-start.8
  273.9 204.7 %reduce-scatter.3.cloned.1.call-start = ((), (), s32[]{:S(2)}) async-start(), calls=%async_computation.5 | async-start | bytes 3649536 | tf_op jit(solution)/shard_map/reduce_scatter | solution.py:150
  275.7 2.7 copy-start.2
  275.7 3.4 copy-start.7
  275.7 3.4 copy-start.14
  279.1 1.0 copy-start.11
  279.1 2.3 copy-start.4
  279.5 0.9 copy-start.12
  287.5 5.5 %copy-start.5 = (f32[640,768]{1,0:T(8,128)S(1)}, f32[640,768]{1,0:T(8,128)}, u32[]{:S(2)}) copy-start(f32[640,768]{1,0:T(8,128)} %reshape.434) | copy-start | bytes 5898244
  287.5 5.5 %copy-start.9 = (bf16[640,768]{1,0:T(8,128)(2,1)S(1)}, bf16[640,768]{1,0:T(8,128)(2,1)}, u32[]{:S(2)}) copy-start(bf16[640,768]{1,0:T(8,128)(2,1)} %all_to_all.32) | copy-start | bytes 2949124
  301.6 70.5 %all-to-all-start.2 = ((bf16[32,2,7680]{2,1,0:T(2,128)(2,1)}), bf16[32,2,7680]{2,1,0:T(2,128)(2,1)}, u32[]{:S(2)}, u32[]{:S(2)}) async-start(bf16[32,2,7680]{2,1,0:T(2,128)(2,1)} %reshape.442), calls=%async_computation.2 | async-start | bytes 1966080 | tf_op jit(solution)/shard_map/all_to_all | solution.py:147
Sparse Core Ops, SparseCore 0:
  274.0 96.5 reduce-scatter.4
  376.0 102.4 reduce-scatter.2
